TPU v7x, 32 devices: a whole 2x2x4 slice. The times are simulated.
32 devices in a mesh: shard: 2 (over x), context: 4 (over y, core), tensor: 4 (over z).
Axes of the slice: x: 2, y: 2, z: 4, core: 2. Of those that a mesh axis runs over, the one named last changes fastest.
Arguments:
- hidden: float32 [2, 1024, 768], P('shard', 'context'), may hold values from -6 to 6
- enc_states: bfloat16 [2, 512, 768], P('shard', 'context'), may hold values from -6 to 6
- cotangent: float32 [2, 1024, 768], P('shard', 'context'), may hold values from -6 to 6
- segments: int32 [2, 1024], P('shard', 'context'), may hold values from 0 to 2, as said below
- positions: int32 [2, 1024], P('shard', 'context'), may hold values from 0 to 623, as said below
- enc_segments: int32 [2, 512], P('shard', 'context'), may hold values from 0 to 2, as said below
- doc_source: int32 [2, 3], P('shard'), may hold values from 0 to 2, each once within a row
- bucket_of: int32 [1024], replicated, may hold values from 0 to 31, as said below
- norm_self: float32 [768], replicated, may hold values from 0.5 to 1.5
- norm_cross: float32 [768], replicated, may hold values from 0.5 to 1.5
- norm_ffn: float32 [768], replicated, may hold values from 0.5 to 1.5
- bias_table: float32 [32, 12], P(None, 'tensor'), may hold values from -5 to 5
- w_q: bfloat16 [768, 768], P('shard', 'tensor'), may hold values from -0.0546875 to 0.0546875
- w_k: bfloat16 [768, 768], P('shard', 'tensor'), may hold values from -0.21875 to 0.21875
- w_v: bfloat16 [768, 768], P('shard', 'tensor'), may hold values from -0.21875 to 0.21875
- w_o: bfloat16 [768, 768], P('tensor', 'shard'), may hold values from -0.875 to 0.875
- c_q: bfloat16 [768, 768], P('shard', 'tensor'), may hold values from -0.0546875 to 0.0546875
- c_k: bfloat16 [768, 768], P('shard', 'tensor'), may hold values from -0.21875 to 0.21875
- c_v: bfloat16 [768, 768], P('shard', 'tensor'), may hold values from -0.21875 to 0.21875
- c_o: bfloat16 [768, 768], P('tensor', 'shard'), may hold values from -0.875 to 0.875
- w_gate: bfloat16 [768, 2048], P('shard', 'tensor'), may hold values from -0.21875 to 0.21875
- w_up: bfloat16 [768, 2048], P('shard', 'tensor'), may hold values from -0.21875 to 0.21875
- w_down: bfloat16 [2048, 768], P('tensor', 'shard'), may hold values from -0.125 to 0.125
Outputs:
- output: float32 [2, 1024, 768], P('shard', 'context')
- d_hidden: float32 [2, 1024, 768], P('shard', 'context')
- d_enc_states: float32 [2, 512, 768], P('shard', 'context')
- d_norm_self: float32 [768], replicated
- d_norm_cross: float32 [768], replicated
- d_norm_ffn: float32 [768], replicated
- d_bias_table: float32 [32, 12], P(None, 'tensor')
- d_w_q: float32 [768, 768], P('shard', 'tensor')
- d_w_k: float32 [768, 768], P('shard', 'tensor')
- d_w_v: float32 [768, 768], P('shard', 'tensor')
- d_w_o: float32 [768, 768], P('tensor', 'shard')
- d_c_q: float32 [768, 768], P('shard', 'tensor')
- d_c_k: float32 [768, 768], P('shard', 'tensor')
- d_c_v: float32 [768, 768], P('shard', 'tensor')
- d_c_o: float32 [768, 768], P('tensor', 'shard')
- d_w_gate: float32 [768, 2048], P('shard', 'tensor')
- d_w_up: float32 [768, 2048], P('shard', 'tensor')
- d_w_down: float32 [2048, 768], P('tensor', 'shard')
Inputs may be any that keep to these rules, and one draw needn't show every extreme that they name: `segments`: in each sequence the document number starts at 0 and rises by one at each new document; there are exactly 3 documents, each a contiguous run of 200 tokens or more. positions count the tokens before this one in its document; some document is 624 tokens long. `enc_segments`: in each sequence the encoder segment number starts at 0 and rises by one at each new segment; exactly 3 segments, each a contiguous run of 64 encoder states or more. `doc_source`: each row is a permutation of 0 to 2. bucket_of is 0 at distance 0, never falls, and is 31 from distance 128 - 1 on.
All inputs are finite; a program needn't handle non-finite values.
Results may differ from a plain program's by a relative error of at most 0.023.
Values may be sent and summed in bfloat16 or wider, within the bound.
A program may use at most 128 MiB of HBM per device.

v0:
```python
import functools
import itertools

import jax
import jax.numpy as jnp
from jax import lax
from jax.experimental import pallas as pl
from jax.experimental.pallas import tpu as pltpu
from jax.sharding import PartitionSpec as P

EPSILON = 1e-06
MASKED = -1e30
MESH = pl.DeviceIdType.MESH
BF16 = jnp.bfloat16
F32 = jnp.float32


def low(values):
    return values.astype(BF16)


def mm(left, right):
    return jnp.dot(left, right, preferred_element_type=F32)


def mm_tn(left, right):
    return lax.dot_general(
        left, right, (((0,), (0,)), ((), ())), preferred_element_type=F32
    )


def mm_nt(left, right):
    return lax.dot_general(
        left, right, (((1,), (1,)), ((), ())), preferred_element_type=F32
    )


def vmem():
    return pl.BlockSpec(memory_space=pltpu.VMEM)


def inv_rms(rows):
    return lax.rsqrt(jnp.mean(rows * rows, axis=-1, keepdims=True) + EPSILON)


def norm_back(rows, gain, grad):
    r = inv_rms(rows)
    weighted = gain * grad
    d_gain = jnp.sum(grad * rows * r, axis=0, keepdims=True)
    d_rows = r * weighted - rows * (r * r * r) * jnp.mean(weighted * rows, axis=-1, keepdims=True)
    return d_rows, d_gain


def offsets_of(mesh_sizes, axes):
    sizes = [mesh_sizes[a] for a in axes]
    return [o for o in itertools.product(*[range(s) for s in sizes]) if any(o)]


class Wire:
    def __init__(self, mesh_sizes, send_sem, recv_sem):
        self.sizes = mesh_sizes
        self.send_sem, self.recv_sem = send_sem, recv_sem
        self.used = 0

    def me(self, axes):
        return tuple(lax.axis_index(a) for a in axes)

    def peers(self, axes):
        mine = self.me(axes)
        return [
            tuple(lax.rem(m + o, self.sizes[a]) for m, o, a in zip(mine, off, axes))
            for off in offsets_of(self.sizes, axes)
        ]

    def barrier(self, axes_list):
        sem = pltpu.get_barrier_semaphore()
        count = 0
        seen = set()
        for axes in axes_list:
            for off in offsets_of(self.sizes, axes):
                key = tuple(sorted((a, o) for a, o in zip(axes, off) if o))
                if key in seen:
                    continue
                seen.add(key)
                ids = {a: lax.rem(lax.axis_index(a) + o, self.sizes[a]) for a, o in key}
                pl.semaphore_signal(sem, inc=1, device_id=ids, device_id_type=MESH)
                count += 1
        pl.semaphore_wait(sem, count)

    def send(self, axes, source, target):
        copies = []
        for k, peer in enumerate(self.peers(axes)):
            copy = pltpu.make_async_remote_copy(
                src_ref=source(peer),
                dst_ref=target(k),
                send_sem=self.send_sem.at[self.used],
                recv_sem=self.recv_sem.at[self.used],
                device_id=dict(zip(axes, peer)),
                device_id_type=MESH,
            )
            copy.start()
            copies.append(copy)
            self.used += 1
        return copies

    def gather(self, axis, source, out):
        mine = lax.axis_index(axis)
        return self.send((axis,), lambda peer: source, lambda k: out.at[mine])

    def scatter(self, axes, source, landing):
        def block(peer):
            ref = source
            for p in peer:
                ref = ref.at[p]
            return ref

        return self.send(axes, block, lambda k: landing.at[k])


def wait_recv(copies):
    for copy in copies:
        copy.wait_recv()


def wait_send(copies):
    for copy in copies:
        copy.wait_send()


def n_peers(mesh_sizes, axes):
    return len(offsets_of(mesh_sizes, axes))


class Plan:
    def __init__(self, sizes, gathers=(), sums=(), main=None):
        self.sizes = sizes
        self.gathers = list(gathers)
        self.sums = list(sums)


def call(cid, sizes, body, inputs, outs, scratch, copies):
    return pl.pallas_call(
        body,
        out_shape=outs,
        in_specs=[vmem()] * len(inputs),
        out_specs=tuple(vmem() for _ in outs),
        scratch_shapes=list(scratch)
        + [pltpu.SemaphoreType.DMA((copies,)), pltpu.SemaphoreType.DMA((copies,))],
        compiler_params=pltpu.CompilerParams(collective_id=cid, has_side_effects=True),
    )(*inputs)


GROUP = ("shard", "context")


def block_sum(source, mine, landing, count):
    own = source
    for m in mine:
        own = own.at[m]
    total = own[...].astype(F32)
    for k in range(count):
        total = total + landing[k].astype(F32)
    return total


def comm(cid, sizes, gathers, sums, reduces, epilogue, extra_in, extra_out, smalls=()):
    ng, ns_, nr, nx = len(gathers), len(sums), len(reduces), len(extra_in)
    inputs = [g for g, _ in gathers] + list(sums) + [r for r, _ in reduces] + list(extra_in)
    inputs += [s for s, _ in smalls]
    nsm = len(smalls)
    outs = [jax.ShapeDtypeStruct((sizes[a],) + g.shape, g.dtype) for g, a in gathers]
    outs += [jax.ShapeDtypeStruct(s.shape[1:], BF16) for s in sums]
    second = [ax for ax, _, _ in (epilogue.second if epilogue else ())]
    outs += [
        jax.ShapeDtypeStruct((sizes[ax],) + shape, dt)
        for ax, shape, dt in (epilogue.second if epilogue else ())
    ]
    outs += list(extra_out)
    outs += [jax.ShapeDtypeStruct(s.shape, F32) for s, _ in smalls]
    group_n = n_peers(sizes, GROUP)
    scratch = [pltpu.VMEM((group_n,) + s.shape[2:], BF16) for s in sums]
    scratch += [pltpu.VMEM((sizes[a] - 1,) + r.shape[1:], r.dtype) for r, a in reduces]
    scratch += [pltpu.VMEM((n_peers(sizes, ax),) + s.shape, F32) for s, ax in smalls]
    copies = sum(sizes[a] - 1 for _, a in gathers)
    copies += ns_ * (group_n + sizes["context"] - 1)
    copies += sum(sizes[a] - 1 for _, a in reduces) + sum(sizes[a] - 1 for a in second)
    copies += sum(n_peers(sizes, ax) for _, ax in smalls)
    axes_list = [(a,) for _, a in gathers] + [(a,) for _, a in reduces] + [(a,) for a in second]
    axes_list += ([GROUP, ("context",)] if ns_ else []) + [ax for _, ax in smalls]
    n_in, n_out = len(inputs), len(outs)

    def body(*refs):
        ins, os_ = refs[:n_in], refs[n_in : n_in + n_out]
        scr, (send_sem, recv_sem) = refs[n_in + n_out : -2], refs[-2:]
        g_in, s_in = ins[:ng], ins[ng : ng + ns_]
        r_in = ins[ng + ns_ : ng + ns_ + nr]
        x_in = ins[ng + ns_ + nr : ng + ns_ + nr + nx]
        sm_in = ins[ng + ns_ + nr + nx :]
        g_out, s_out = os_[:ng], os_[ng : ng + ns_]
        e_out = os_[ng + ns_ : ng + ns_ + len(second)]
        x_out = os_[ng + ns_ + len(second) : n_out - nsm]
        sm_out = os_[n_out - nsm :]
        s_land, r_land, sm_land = scr[:ns_], scr[ns_ : ns_ + nr], scr[ns_ + nr :]
        wire = Wire(sizes, send_sem, recv_sem)
        wire.barrier(axes_list)
        pending, recvs = [], []
        r_copies = [
            wire.scatter((a,), ref, land) for ref, land, (_, a) in zip(r_in, r_land, reduces)
        ]
        s_copies = [wire.scatter(GROUP, ref, land) for ref, land in zip(s_in, s_land)]
        for ref, out, (_, a) in zip(g_in, g_out, gathers):
            c = wire.gather(a, ref, out)
            pending += c
            recvs += c
        for ref, out, (_, a) in zip(g_in, g_out, gathers):
            out[lax.axis_index(a)] = ref[...]
        totals = []
        for ref, land, c, (_, a) in zip(r_in, r_land, r_copies, reduces):
            wait_recv(c)
            totals.append(block_sum(ref, (lax.axis_index(a),), land, sizes[a] - 1))
            pending += c
        if epilogue is not None:
            blocks = epilogue.run(totals, x_in, x_out)
            for block, out, ax in zip(blocks, e_out, second):
                mine = lax.axis_index(ax)
                out[mine] = block
                c = wire.gather(ax, out.at[mine], out)
                pending += c
                recvs += c
        mine_c = lax.axis_index("context")
        for ref, land, c, out in zip(s_in, s_land, s_copies, s_out):
            wait_recv(c)
            pending += c
            total = block_sum(ref, (lax.axis_index("shard"), mine_c), land, group_n)
            out[mine_c] = low(total)
            c2 = wire.gather("context", out.at[mine_c], out)
            pending += c2
            recvs += c2
        for i, (_, axes) in enumerate(smalls):
            source = sm_in[i]
            land = sm_land[i]
            if epilogue is not None and epilogue.small_fill is not None:
                source = epilogue.small_fill(i, sm_in, x_out, sm_out)
            c = wire.send(axes, lambda peer, src=source: src, lambda k, l=land: l.at[k])
            wait_recv(c)
            wait_send(c)
            total = source[...]
            for k in range(len(c)):
                total = total + land[k]
            sm_out[i][...] = total
        wait_recv(recvs)
        wait_send(pending)

    return call(cid, sizes, body, inputs, outs, scratch, copies)


class Epilogue:
    def __init__(self, second, run, small_fill=None):
        self.second, self.run, self.small_fill = second, run, small_fill


def self_fwd_kernel(heads, dh, q, kv, seg_q, seg_k, line, mixed, probs):
    rows, span = probs.shape[1:]
    width = heads * dh
    first = lax.axis_index("context") * rows
    t = first + lax.broadcasted_iota(jnp.int32, (rows, span), 0)
    u = lax.broadcasted_iota(jnp.int32, (rows, span), 1)
    allowed = (u <= t) & (seg_q[...] == seg_k[...])
    for h in range(heads):
        cols = slice(h * dh, (h + 1) * dh)
        bias = pltpu.roll(
            jnp.broadcast_to(line[h : h + 1, :], (rows, span)), 0, 1, stride=1, stride_axis=0
        )
        s = mm_nt(q[:, cols], kv[:, cols]) + bias
        s = jnp.where(allowed, s, MASKED)
        e = jnp.exp(s - jnp.max(s, axis=1, keepdims=True))
        p = e / jnp.sum(e, axis=1, keepdims=True)
        probs[h] = p
        mixed[:, cols] = low(mm(low(p), kv[:, width + h * dh : width + (h + 1) * dh]))


def cross_fwd_kernel(heads, dh, q, kv, seg_q, seg_k, mixed, probs):
    width = heads * dh
    allowed = seg_q[...] == seg_k[...]
    for h in range(heads):
        cols = slice(h * dh, (h + 1) * dh)
        s = jnp.where(allowed, mm_nt(q[:, cols], kv[:, cols]), MASKED)
        e = jnp.exp(s - jnp.max(s, axis=1, keepdims=True))
        p = e / jnp.sum(e, axis=1, keepdims=True)
        probs[h] = p
        mixed[:, cols] = low(mm(low(p), kv[:, width + h * dh : width + (h + 1) * dh]))


def back_kernel(heads, dh, with_bias, q, kv, probs, g, dq, dkv, *diag):
    rows, span = probs.shape[1:]
    width = heads * dh
    if with_bias:
        a = lax.broadcasted_iota(jnp.int32, (rows, rows), 0)
        b = lax.broadcasted_iota(jnp.int32, (rows, rows), 1)
        flip = jnp.where(a + b == rows - 1, 1.0, 0.0).astype(BF16)
        diag[0][...] = jnp.zeros_like(diag[0])
    for h in range(heads):
        cols = slice(h * dh, (h + 1) * dh)
        vcols = slice(width + h * dh, width + (h + 1) * dh)
        p = probs[h]
        dp = mm_nt(g[:, cols], kv[:, vcols])
        ds = low(p * (dp - jnp.sum(dp * p, axis=1, keepdims=True)))
        dq[:, cols] = low(mm(ds, kv[:, cols]))
        dkv[:, cols] = low(mm_tn(ds, q[:, cols]))
        dkv[:, vcols] = low(mm_tn(low(p), g[:, cols]))
        if with_bias:
            skew = pltpu.roll(mm(flip, ds), 0, 1, stride=1, stride_axis=0)
            diag[0][h : h + 1, :] = jnp.sum(skew, axis=0, keepdims=True)


def local_call(kernel, inputs, outs):
    return pl.pallas_call(
        kernel,
        out_shape=outs,
        in_specs=[vmem()] * len(inputs),
        out_specs=tuple(vmem() for _ in outs),
    )(*inputs)


def sds(shape, dtype):
    return jax.ShapeDtypeStruct(shape, dtype)


def body(
    sizes,
    hidden,
    enc_states,
    cotangent,
    segments,
    positions,
    enc_segments,
    doc_source,
    bucket_of,
    norm_self,
    norm_cross,
    norm_ffn,
    bias_table,
    w_q,
    w_k,
    w_v,
    w_o,
    c_q,
    c_k,
    c_v,
    c_o,
    w_gate,
    w_up,
    w_down,
):
    ns, nc, nt = sizes["shard"], sizes["context"], sizes["tensor"]
    seq_count, rows, width = hidden.shape
    assert seq_count == 1
    enc_len = enc_states.shape[1]
    heads = bias_table.shape[1]
    unit = w_q.shape[1]
    dh = unit // heads
    ffn = w_gate.shape[1]
    span = nc * rows
    enc_span = nc * enc_len
    ctx = lax.axis_index("context")
    part = rows // nt
    comm_ = functools.partial(comm, sizes=sizes)

    x = hidden[0]
    cot = cotangent[0]
    enc = enc_states[0]
    gain_s, gain_c, gain_f = norm_self[None, :], norm_cross[None, :], norm_ffn[None, :]

    pack_a = jnp.concatenate([w_q, w_k, w_v, c_k], axis=1)
    pack_b = jnp.concatenate([c_v, c_q], axis=1)
    segs = jnp.concatenate([segments, enc_segments], axis=1)
    a_all, b_all, seg_all = comm_(
        0,
        gathers=[(pack_a, "shard"), (pack_b, "shard"), (segs, "context")],
        sums=[], reduces=[], epilogue=None, extra_in=[], extra_out=[],
    )
    a_all = a_all.reshape(width, 4 * unit)
    b_all = b_all.reshape(width, 2 * unit)
    wq, wk, wv, ck = (a_all[:, i * unit : (i + 1) * unit] for i in range(4))
    cv, cq = b_all[:, :unit], b_all[:, unit:]
    seg_k = seg_all[:, 0, :rows].reshape(1, span)
    enc_seg_k = seg_all[:, 0, rows:].reshape(1, enc_span)
    seg_q = segments.reshape(rows, 1)
    target = jnp.zeros_like(segments)
    for doc in range(doc_source.shape[1]):
        target = jnp.where(segments == doc, doc_source[:, doc : doc + 1], target)
    target = target.reshape(rows, 1)

    normed_self = low(x * inv_rms(x) * gain_s)
    qkv = low(mm(normed_self, a_all[:, : 3 * unit]))
    q = qkv[:, :unit]
    ekv_own = jnp.concatenate([low(mm(enc, ck)), low(mm(enc, cv))], axis=1)
    kv_all, ekv_all, wo_all, co_all = comm_(
        1,
        gathers=[(qkv[:, unit:], "context"), (ekv_own, "context"), (w_o, "shard"), (c_o, "shard")],
        sums=[], reduces=[], epilogue=None, extra_in=[], extra_out=[],
    )
    kv = kv_all.reshape(span, 2 * unit)
    ekv = ekv_all.reshape(enc_span, 2 * unit)
    wo = jnp.moveaxis(wo_all, 0, 1).reshape(unit, width)
    co = jnp.moveaxis(co_all, 0, 1).reshape(unit, width)

    flipped = bucket_of[::-1]
    twice = jnp.concatenate([flipped, flipped])
    bucket = lax.dynamic_slice(twice, (span - ctx * rows - 1,), (span,))
    onehot = (bucket[None, :] == jnp.arange(bias_table.shape[0], dtype=jnp.int32)[:, None]).astype(F32)
    line = lax.dot_general(
        bias_table, onehot, (((0,), (0,)), ((), ())), precision=lax.Precision.HIGHEST
    )
    mixed, probs = local_call(
        functools.partial(self_fwd_kernel, heads, dh),
        [q, kv, seg_q, seg_k, line],
        [sds((rows, unit), BF16), sds((heads, rows, span), F32)],
    )

    def fwd_step(totals, x_in, x_out):
        rows_in, gain = x_in
        base = rows_in[lax.axis_index("tensor")] if len(rows_in.shape) == 3 else rows_in[...]
        after = base + totals[0]
        x_out[0][...] = after
        return [low(after * inv_rms(after) * gain[...])]

    shape3 = (part, width)
    ep_fwd = Epilogue([("tensor", shape3, BF16)], fwd_step)
    part_self = low(mm(mixed, wo)).reshape(nt, part, width)
    gate_all, up_all, normed_cross, after_self = comm_(
        2,
        gathers=[(w_gate, "shard"), (w_up, "shard")],
        sums=[], reduces=[(part_self, "tensor")], epilogue=ep_fwd,
        extra_in=[x.reshape(nt, part, width), gain_c], extra_out=[sds(shape3, F32)],
    )
    wg, wu = gate_all.reshape(width, ffn), up_all.reshape(width, ffn)
    normed_cross = normed_cross.reshape(rows, width)

    cqs = low(mm(normed_cross, cq))
    cmixed, cprobs = local_call(
        functools.partial(cross_fwd_kernel, heads, dh),
        [cqs, ekv, target, enc_seg_k],
        [sds((rows, unit), BF16), sds((heads, rows, enc_span), F32)],
    )
    part_cross = low(mm(cmixed, co)).reshape(nt, part, width)
    down_all, normed_ffn, after_cross = comm_(
        3,
        gathers=[(w_down, "shard")],
        sums=[], reduces=[(part_cross, "tensor")], epilogue=ep_fwd,
        extra_in=[after_self, gain_f], extra_out=[sds(shape3, F32)],
    )
    wd = jnp.moveaxis(down_all, 0, 1).reshape(ffn, width)
    normed_ffn = normed_ffn.reshape(rows, width)

    gate_pre, up_pre = mm(normed_ffn, wg), mm(normed_ffn, wu)
    top_low = low(cot)
    d_units = mm_nt(top_low, wd)
    k0, k1 = 0.7978845608028654, 0.044715
    sq = gate_pre * gate_pre
    th = jnp.tanh(k0 * (gate_pre + k1 * gate_pre * sq))
    gelu = 0.5 * gate_pre * (1.0 + th)
    d_gelu = 0.5 * (1.0 + th) + 0.5 * gate_pre * (1.0 - th * th) * k0 * (1.0 + 3.0 * k1 * sq)
    units = low(gelu * up_pre)
    d_gate = low(d_units * up_pre * d_gelu)
    d_up = low(d_units * gelu)
    part_out = low(mm(units, wd)).reshape(nt, part, width)
    part_ffn = low(mm_nt(d_gate, wg) + mm_nt(d_up, wu)).reshape(nt, part, width)

    def wide(grad):
        return low(grad).reshape(ns, nc, width // (ns * nc), grad.shape[1])

    def tall(grad):
        r, c = grad.shape
        return jnp.moveaxis(low(grad).reshape(nc, r // nc, ns, c // ns), 2, 0)

    g_down = tall(mm_tn(units, top_low))
    g_gate = wide(mm_tn(normed_ffn, d_gate))
    g_up = wide(mm_tn(normed_ffn, d_up))

    def back_step(totals, x_in, x_out):
        rows_in, gain, above = x_in
        over = above[lax.axis_index("tensor")] if len(above.shape) == 3 else above[...]
        d_rows, d_gain = norm_back(rows_in[...], gain[...], totals[0])
        grad = over + d_rows
        x_out[0][...] = grad
        x_out[1][...] = d_gain
        return [low(grad)]

    ep_back = Epilogue([("tensor", shape3, BF16)], back_step)
    back_out = [sds(shape3, F32), sds((1, width), F32)]
    down_sum, cross_low_grad, cross_grad, dg_ffn = comm_(
        4,
        gathers=[], sums=[g_down], reduces=[(part_ffn, "tensor")], epilogue=ep_back,
        extra_in=[after_cross, gain_f, cot.reshape(nt, part, width)], extra_out=back_out,
    )
    cross_low_grad = cross_low_grad.reshape(rows, width)
    d_cmixed = low(mm_nt(cross_low_grad, co))
    d_cq, d_ekv = local_call(
        functools.partial(back_kernel, heads, dh, False),
        [cqs, ekv, cprobs, d_cmixed],
        [sds((rows, unit), BF16), sds((enc_span, 2 * unit), BF16)],
    )
    part_ncross = low(mm_nt(d_cq, cq)).reshape(nt, part, width)

    def cross_back_step(totals, x_in, x_out):
        x_out[2][...] = low(totals[1])
        return back_step(totals, x_in, x_out)

    gate_sum, up_sum, self_low_grad, self_grad, dg_cross, d_ekv_own = comm_(
        5,
        gathers=[], sums=[g_gate, g_up],
        reduces=[
            (part_ncross, "tensor"),
            (d_ekv.reshape(nc, enc_len, 2 * unit), "context"),
        ],
        epilogue=Epilogue([("tensor", shape3, BF16)], cross_back_step),
        extra_in=[after_self, gain_c, cross_grad],
        extra_out=back_out + [sds((enc_len, 2 * unit), BF16)],
    )
    self_low_grad = self_low_grad.reshape(rows, width)
    d_mixed = low(mm_nt(self_low_grad, wo))
    d_q, d_kv, diag = local_call(
        functools.partial(back_kernel, heads, dh, True),
        [q, kv, probs, d_mixed],
        [sds((rows, unit), BF16), sds((span, 2 * unit), BF16), sds((8, span), F32)],
    )

    g_co = tall(mm_tn(cmixed, cross_low_grad))
    g_wo = tall(mm_tn(mixed, self_low_grad))
    g_cq = mm_tn(normed_cross, d_cq)
    g_ckv = mm_tn(enc, d_ekv_own)
    g_cross = wide(jnp.concatenate([g_cq, g_ckv], axis=1))
    d_ek, d_ev = d_ekv_own[:, :unit], d_ekv_own[:, unit:]
    part_enc = low(mm_nt(d_ek, ck) + mm_nt(d_ev, cv)).reshape(nt, enc_len // nt, width)

    def mid_step(totals, x_in, x_out):
        base = x_in[0][...] - x_in[1][lax.axis_index("tensor")]
        x_out[0][...] = low(totals[0])
        return [low(totals[1] + base), low(totals[2])]

    co_sum, wo_sum, cross_sum, out_delta, d_enc, d_kv_own = comm_(
        6,
        gathers=[], sums=[g_co, g_wo, g_cross],
        reduces=[
            (d_kv.reshape(nc, rows, 2 * unit), "context"),
            (part_out, "tensor"),
            (part_enc, "tensor"),
        ],
        epilogue=Epilogue(
            [("tensor", shape3, BF16), ("tensor", (enc_len // nt, width), BF16)], mid_step
        ),
        extra_in=[after_cross, x.reshape(nt, part, width)],
        extra_out=[sds((rows, 2 * unit), BF16)],
    )
    d_qkv = jnp.concatenate([d_q, d_kv_own], axis=1)
    part_nself = low(mm_nt(d_qkv, a_all[:, : 3 * unit])).reshape(nt, part, width)
    g_self = wide(mm_tn(normed_self, d_qkv))

    lane = jnp.arange(span, dtype=jnp.int32)
    dist = lax.rem(ctx * rows + (rows - 1) - lane + span, span)
    del dist
    bucket_d = lax.dynamic_slice(twice, (lax.rem(2 * span - ctx * rows - rows, span),), (span,))
    onehot_d = (bucket_d[None, :] == jnp.arange(bias_table.shape[0], dtype=jnp.int32)[:, None]).astype(F32)
    g_bias = lax.dot_general(
        diag, onehot_d, (((1,), (1,)), ((), ())), precision=lax.Precision.HIGHEST
    )

    def last_step(totals, x_in, x_out):
        rows_in, gain, above, cot_in, dgf, dgc = x_in
        d_rows, d_gain = norm_back(rows_in[lax.axis_index("tensor")], gain[...], totals[0])
        x_out[0][0:1, :] = dgf[...]
        x_out[0][1:2, :] = dgc[...]
        x_out[0][2:3, :] = d_gain
        x_out[0][3:8, :] = jnp.zeros_like(x_out[0][3:8, :])
        return [low(above[...] - cot_in[lax.axis_index("tensor")] + d_rows)]

    def small_fill(i, sm_in, x_out, sm_out):
        return [sm_in[0], x_out[0], sm_out[1]][i]

    gains0 = jnp.zeros((8, width), F32)
    self_sum, hid_delta, _, bias_sum, _, gain_sum = comm_(
        7,
        gathers=[], sums=[g_self], reduces=[(part_nself, "tensor")],
        epilogue=Epilogue([("tensor", shape3, BF16)], last_step, small_fill),
        extra_in=[
            x.reshape(nt, part, width), gain_s, self_grad, cot.reshape(nt, part, width),
            dg_ffn, dg_cross,
        ],
        extra_out=[sds((8, width), F32)],
        smalls=[(g_bias, GROUP), (gains0, ("tensor",)), (gains0, GROUP)],
    )

    def wide_out(total):
        return total.reshape(width // ns, total.shape[-1]).astype(F32)

    def tall_out(total):
        return total.reshape(total.shape[0] * total.shape[1], total.shape[2]).astype(F32)

    self_w, cross_w = wide_out(self_sum), wide_out(cross_sum)
    return (
        (x + out_delta.reshape(rows, width).astype(F32))[None],
        (cot + hid_delta.reshape(rows, width).astype(F32))[None],
        d_enc.reshape(1, enc_len, width).astype(F32),
        gain_sum[2],
        gain_sum[1],
        gain_sum[0],
        bias_sum[:heads].T,
        self_w[:, :unit],
        self_w[:, unit : 2 * unit],
        self_w[:, 2 * unit :],
        tall_out(wo_sum),
        cross_w[:, :unit],
        cross_w[:, unit : 2 * unit],
        cross_w[:, 2 * unit :],
        tall_out(co_sum),
        wide_out(gate_sum),
        wide_out(up_sum),
        tall_out(down_sum),
    )


def solution(mesh):
    tok = P("shard", "context", None)
    ids = P("shard", "context")
    wide, tall = P("shard", "tensor"), P("tensor", "shard")
    in_specs = (tok, tok, tok, ids, ids, ids, P("shard", None), P(), P(), P(), P(), P(None, "tensor"))
    in_specs += (wide, wide, wide, tall) * 2 + (wide, wide, tall)
    out_specs = (tok, tok, tok, P(), P(), P(), P(None, "tensor"))
    out_specs += (wide, wide, wide, tall) * 2 + (wide, wide, tall)
    sizes = {a: mesh.shape[a] for a in ("shard", "context", "tensor")}
    return jax.shard_map(
        functools.partial(body, sizes),
        mesh=mesh,
        in_specs=in_specs,
        out_specs=out_specs,
        check_vma=False,
    )
```

profile of v0, /device:TPU:0, one launch (start us, length us, event | category | flops | bytes accessed | tf_op | source)
XLA Modules:
  0.0 326.7 jit_solution(16669005494765317239)
XLA Ops:
  1.6 1.5 convolution_bitcast_fusion.1.line
  9.3 27.0 %shard_map.349 = (bf16[2,384,768]{2,1,0:T(8,128)(2,1)}, bf16[2,384,384]{2,1,0:T(8,128)(2,1)}, s32[4,1,384]{2,1,0:T(1,128)}) custom-call(bf16[384,768]{1,0:T(8,128)(2,1)} %pad_maximum_fusion.1.refs_0_, bf16[384,384]{1,0:T(8,128)(2,1)} %pad_maximum_fusion.3.refs_1_, s32[1,384]{1,0:T(1,128)} %pad_add_fusion.refs_2_), custom_call_target="tpu_custom_call" | custom-call | tf_op jit(solution)/shard_map/pallas_call | solution.py:142
  36.3 1.5 convolution_convert_fusion.18
  38.0 1.3 convolution_convert_fusion.17
  41.6 16.5 %shard_map.350 = (bf16[4,256,384]{2,1,0:T(8,128)(2,1)}, bf16[4,128,384]{2,1,0:T(8,128)(2,1)}, bf16[2,192,384]{2,1,0:T(8,128)(2,1)}, bf16[2,192,384]{2,1,0:T(8,128)(2,1)}) custom-call(bf16[256,384]{1,0:T(8,128)(2,1)} %slice.95.refs_0_, bf16[128,384]{1,0:T(8,128)(2,1)} %pad_maximum_fusion.6.refs_1_, bf16[192,384]{1,0:T(8,128)(2,1)} %refs_2_.1, ...), custom_call_target="tpu_custom_call" | custom-call | tf_op jit(solution)/shard_map/pallas_call | solution.py:142
  60.3 5.3 %shard_map.351 = (bf16[256,192]{1,0:T(8,128)(2,1)}, f32[3,256,1024]{2,1,0:T(8,128)}) custom-call(bf16[256,192]{1,0:T(8,128)(2,1)} %slice.94.q, bf16[1024,384]{1,0:T(8,128)(2,1)} %bitcast.168, s32[256,1]{1,0:T(8,128)} %copy.103.seg_q, s32[1,1024]{1,0:T(1,128)} %bitcast.220, f32[3,1024]{1,0:T(4,128)} %convolution_bitcast_fusion.1.line), custom_call_target="tpu_custom_call" | custom-call | tf_op jit(solution)/shard_map/pallas_call | solution.py:317
  66.3 1.9 convolution_convert_fusion.10
  68.8 25.3 %shard_map.352 = (bf16[2,384,512]{2,1,0:T(8,128)(2,1)}, bf16[2,384,512]{2,1,0:T(8,128)(2,1)}, bf16[4,64,768]{2,1,0:T(8,128)(2,1)}, f32[64,768]{1,0:T(8,128)}) custom-call(bf16[384,512]{1,0:T(8,128)(2,1)} %refs_0_.2, bf16[384,512]{1,0:T(8,128)(2,1)} %refs_1_.1, bf16[4,64,768]{2,1,0:T(8,128)(2,1)} %bitcast.190, f32[4,64,768]{2,1,0:T(8,128)} %bitcast.158, ...), custom_call_target="tpu_custom_call" | custom-call | tf_op jit(solution)/shard_map/pallas_call | solution.py:142
  94.1 2.1 convolution_convert_fusion.14.q
  96.8 1.9 fusion.30
  100.1 4.0 %shard_map.353 = (bf16[256,192]{1,0:T(8,128)(2,1)}, f32[3,256,512]{2,1,0:T(8,128)}) custom-call(bf16[256,192]{1,0:T(8,128)(2,1)} %convolution_convert_fusion.14.q, bf16[512,384]{1,0:T(8,128)(2,1)} %bitcast.193, s32[256,1]{1,0:T(8,128)} %copy.106.seg_q, s32[1,512]{1,0:T(1,128)} %slice_bitcast_fusion.1.seg_k), custom_call_target="tpu_custom_call" | custom-call | tf_op jit(solution)/shard_map/pallas_call | solution.py:317
  104.8 1.9 convolution_convert_fusion.9
  107.3 23.5 %shard_map.354 = (bf16[2,512,384]{2,1,0:T(8,128)(2,1)}, bf16[4,64,768]{2,1,0:T(8,128)(2,1)}, f32[64,768]{1,0:T(8,128)}) custom-call(bf16[512,384]{1,0:T(8,128)(2,1)} %refs_0_.3, bf16[4,64,768]{2,1,0:T(8,128)(2,1)} %bitcast.188, f32[64,768]{1,0:T(8,128)} %get-tuple-element.71.refs_2_.refs_4_, f32[1,768]{1,0:T(1,128)} %broadcast_in_dim.50.refs_3_), custom_call_target="tpu_custom_call" | custom-call | tf_op jit(solution)/shard_map/pallas_call | solution.py:142
  130.8 2.2 fusion.39
  139.6 24.2 %shard_map.355 = (bf16[4,128,384]{2,1,0:T(8,128)(2,1)}, bf16[4,64,768]{2,1,0:T(8,128)(2,1)}, f32[64,768]{1,0:T(8,128)}, f32[1,768]{1,0:T(1,128)}) custom-call(bf16[2,4,128,384]{3,2,1,0:T(8,128)(2,1)} %bitcast.172, bf16[4,64,768]{2,1,0:T(8,128)(2,1)} %bitcast.192, f32[64,768]{1,0:T(8,128)} %get-tuple-element.76.refs_2_.refs_6_, ...), custom_call_target="tpu_custom_call" | custom-call | tf_op jit(solution)/shard_map/pallas_call | solution.py:142
  163.8 1.3 convolution_convert_fusion.16
  165.9 4.4 %shard_map.356 = (bf16[256,192]{1,0:T(8,128)(2,1)}, bf16[512,384]{1,0:T(8,128)(2,1)}) custom-call(bf16[256,192]{1,0:T(8,128)(2,1)} %convolution_convert_fusion.14.q, bf16[512,384]{1,0:T(8,128)(2,1)} %bitcast.194, f32[3,256,512]{2,1,0:T(8,128)} %get-tuple-element.78.probs, bf16[256,192]{1,0:T(8,128)(2,1)} %copy.112.g), custom_call_target="tpu_custom_call" | custom-call | tf_op jit(solution)/shard_map/pallas_call | solution.py:317
  170.3 2.1 convolution_convert_fusion.8
  172.3 1.3 convolution_convert_fusion.1
  173.6 1.3 convolution_convert_fusion.2
  174.9 36.6 %shard_map.357 = (bf16[4,96,512]{2,1,0:T(8,128)(2,1)}, bf16[4,96,512]{2,1,0:T(8,128)(2,1)}, bf16[4,64,768]{2,1,0:T(8,128)(2,1)}, f32[64,768]{1,0:T(8,128)}, f32[1,768]{1,0:T(1,128)}, /*index=5*/bf16[128,384]{1,0:T(8,128)(2,1)}) custom-call(bf16[2,4,96,512]{3,2,1,0:T(8,128)(2,1)} %bitcast.178, bf16[2,4,96,512]{3,2,1,0:T(8,128)(2,1)} %bitcast.177, ...), custom_call_target="tpu_custom_call" | custom-call | tf_op jit(solution)/shard_map/pallas_call | solution.py:142
  211.5 2.5 bitcast_convert_fusion.3
  214.0 1.4 fusion.14
  218.7 6.4 %shard_map.358 = (bf16[256,192]{1,0:T(8,128)(2,1)}, bf16[1024,384]{1,0:T(8,128)(2,1)}, f32[8,1024]{1,0:T(8,128)}) custom-call(bf16[256,192]{1,0:T(8,128)(2,1)} %slice.94.q, bf16[1024,384]{1,0:T(8,128)(2,1)} %bitcast.169, f32[3,256,1024]{2,1,0:T(8,128)} %get-tuple-element.84.probs, bf16[256,192]{1,0:T(8,128)(2,1)} %copy.117.g), custom_call_target="tpu_custom_call" | custom-call | tf_op jit(solution)/shard_map/pallas_call | solution.py:317
  226.2 1.4 pad_maximum_fusion.refs_2_
  229.8 40.6 %shard_map.359 = (bf16[4,48,384]{2,1,0:T(8,128)(2,1)}, bf16[4,48,384]{2,1,0:T(8,128)(2,1)}, bf16[4,96,576]{2,1,0:T(8,128)(2,1)}, bf16[4,64,768]{2,1,0:T(8,128)(2...) custom-call(bf16[2,4,48,384]{3,2,1,0:T(8,128)(2,1)} %bitcast.197, bf16[2,4,48,384]{3,2,1,0:T(8,128)(2,1)} %bitcast.196, ...), custom_call_target="tpu_custom_call" | custom-call | tf_op jit(solution)/shard_map/pallas_call | solution.py:142
  270.4 1.8 bitcast_convert_fusion.6
  272.3 2.3 convolution_convert_fusion.5
  275.2 1.6 copy.118
  278.7 34.9 %shard_map.360 = (bf16[4,96,576]{2,1,0:T(8,128)(2,1)}, bf16[4,64,768]{2,1,0:T(8,128)(2,1)}, f32[8,768]{1,0:T(8,128)}, f32[8,32]{1,0:T(8,128)}, f32[8,768]{1,0:T(8,128)}, /*index=5*/f32[8,768]{1,0:T(8,128)}) custom-call(bf16[2,4,96,576]{3,2,1,0:T(8,128)(2,1)} %bitcast.167, bf16[4,64,768]{2,1,0:T(8,128)(2,1)} %bitcast.207, f32[4,64,768]{2,1,0:T(8,128)} %bitcast.160, ...), custom_call_target="tpu_custom_call" | custom-call | tf_op jit(solution)/shard_map/pallas_call | solution.py:142
  317.6 2.3 convert_add_fusion
  319.9 1.5 slice_reduce_fusion
  (174 shorter events, 41.6 us)
Async XLA Ops:
  0.7 35.7 %copy-start = (bf16[1,128,768]{2,1,0:T(8,128)(2,1)S(1)}, bf16[1,128,768]{2,1,0:T(8,128)(2,1)}, u32[]{:S(2)}) copy-start(bf16[1,128,768]{2,1,0:T(8,128)(2,1)} %param.24) | copy-start | bytes 589828
  0.7 5.6 %copy-start.38 = (bf16[384,192]{0,1:T(8,128)(2,1)S(1)}, bf16[384,192]{0,1:T(8,128)(2,1)}, u32[]{:S(2)}) copy-start(bf16[384,192]{0,1:T(8,128)(2,1)} %param.39) | copy-start | bytes 442372
  4.1 3.5 %copy-start.39 = (bf16[384,192]{0,1:T(8,128)(2,1)S(1)}, bf16[384,192]{0,1:T(8,128)(2,1)}, u32[]{:S(2)}) copy-start(bf16[384,192]{0,1:T(8,128)(2,1)} %param.40) | copy-start | bytes 442372
  9.3 30.9 %copy-start.1 = (f32[1,256,768]{2,1,0:T(8,128)S(1)}, f32[1,256,768]{2,1,0:T(8,128)}, u32[]{:S(2)}) copy-start(f32[1,256,768]{2,1,0:T(8,128)} %param.23) | copy-start | bytes 2359300
  36.3 4.0 %copy-start.42 = (bf16[2,384,768]{2,1,0:T(8,128)(2,1)S(1)}, bf16[2,384,768]{2,1,0:T(8,128)(2,1)}, u32[]{:S(2)}) copy-start(bf16[2,384,768]{2,1,0:T(8,128)(2,1)} %get-tuple-element.61) | copy-start | bytes 3538948
  36.3 4.0 %copy-start.45 = (f32[768]{0:T(1024)S(1)}, f32[768]{0:T(1024)}, u32[]{:S(2)}) copy-start(f32[768]{0:T(1024)} %param.30) | copy-start | bytes 9220
  40.8 18.0 %copy-start.47 = (s32[4,1,384]{2,1,0:T(1,128)S(1)}, s32[4,1,384]{2,1,0:T(1,128)}, u32[]{:S(2)}) copy-start(s32[4,1,384]{2,1,0:T(1,128)} %get-tuple-element.64) | copy-start | bytes 18436
  58.2 7.4 %copy-start.35 = (bf16[2,192,384]{2,1,0:T(8,128)(2,1)S(1)}, bf16[2,192,384]{2,1,0:T(8,128)(2,1)}, u32[]{:S(2)}) copy-start(bf16[2,192,384]{2,1,0:T(8,128)(2,1)} %get-tuple-element.66) | copy-start | bytes 884740
  60.3 8.0 %copy-start.49 = (f32[768]{0:T(1024)S(1)}, f32[768]{0:T(1024)}, u32[]{:S(2)}) copy-start(f32[768]{0:T(1024)} %param.31) | copy-start | bytes 9220
  68.2 25.9 %copy-start.16 = (bf16[2,384,384]{2,1,0:T(8,128)(2,1)S(1)}, bf16[2,384,384]{2,1,0:T(8,128)(2,1)}, u32[]{:S(2)}) copy-start(bf16[2,384,384]{2,1,0:T(8,128)(2,1)} %get-tuple-element.62) | copy-start | bytes 1769476
  68.8 27.4 %copy-start.48 = (s32[1,3]{1,0:T(1,128)S(1)}, s32[1,3]{1,0:T(1,128)}, u32[]{:S(2)}) copy-start(s32[1,3]{1,0:T(1,128)} %param.28) | copy-start | bytes 40
  94.1 10.0 %copy-start.34 = (bf16[2,192,384]{2,1,0:T(8,128)(2,1)S(1)}, bf16[2,192,384]{2,1,0:T(8,128)(2,1)}, u32[]{:S(2)}) copy-start(bf16[2,192,384]{2,1,0:T(8,128)(2,1)} %get-tuple-element.70) | copy-start | bytes 884740
  96.2 10.5 %copy-start.50 = (f32[768]{0:T(1024)S(1)}, f32[768]{0:T(1024)}, u32[]{:S(2)}) copy-start(f32[768]{0:T(1024)} %param.32) | copy-start | bytes 9220
  104.1 26.8 %copy-start.8 = (bf16[2,384,512]{2,1,0:T(8,128)(2,1)S(1)}, bf16[2,384,512]{2,1,0:T(8,128)(2,1)}, u32[]{:S(2)}) copy-start(bf16[2,384,512]{2,1,0:T(8,128)(2,1)} %get-tuple-element.74) | copy-start | bytes 2359300
  135.4 2.6 copy-start.20
  135.4 2.6 copy-start.22
  135.4 2.6 copy-start.18
  139.6 24.2 %copy-start.13 = (bf16[2,24,8,384]{3,2,0,1:T(8,128)(2,1)S(1)}, bf16[2,24,8,384]{3,2,0,1:T(8,128)(2,1)}, u32[]{:S(2)}) copy-start(bf16[2,24,8,384]{3,2,0,1:T(8,128)(2,1)} %copy-done.12) | copy-start | bytes 884740
  165.1 5.1 %copy-start.17 = (bf16[2,384,384]{2,1,0:T(8,128)(2,1)S(1)}, bf16[2,384,384]{2,1,0:T(8,128)(2,1)}, u32[]{:S(2)}) copy-start(bf16[2,384,384]{2,1,0:T(8,128)(2,1)} %get-tuple-element.62) | copy-start | bytes 1769476
  165.9 6.5 %copy-start.23 = (bf16[256,512]{1,0:T(8,128)(2,1)S(1)}, bf16[256,512]{1,0:T(8,128)(2,1)}, u32[]{:S(2)}) copy-start(bf16[256,512]{1,0:T(8,128)(2,1)} %copy-done.22) | copy-start | bytes 786436
  170.3 3.4 %copy-start.21 = (bf16[256,512]{1,0:T(8,128)(2,1)S(1)}, bf16[256,512]{1,0:T(8,128)(2,1)}, u32[]{:S(2)}) copy-start(bf16[256,512]{1,0:T(8,128)(2,1)} %copy-done.20) | copy-start | bytes 786436
  218.7 6.4 %copy-start.31 = (bf16[4,64,768]{2,1,0:T(8,128)(2,1)S(1)}, bf16[4,64,768]{2,1,0:T(8,128)(2,1)}, u32[]{:S(2)}) copy-start(bf16[4,64,768]{2,1,0:T(8,128)(2,1)} %get-tuple-element.67) | copy-start | bytes 1179652
  218.7 6.6 %copy-start.28 = (bf16[256,192]{1,0:T(8,128)(2,1)S(1)}, bf16[256,192]{1,0:T(8,128)(2,1)}, u32[]{:S(2)}) copy-start(bf16[256,192]{1,0:T(8,128)(2,1)} %get-tuple-element.79) | copy-start | bytes 294916
  229.8 42.4 %copy-start.41 = (bf16[256,192]{1,0:T(8,128)(2,1)S(1)}, bf16[256,192]{1,0:T(8,128)(2,1)}, u32[]{:S(2)}) copy-start(bf16[256,192]{1,0:T(8,128)(2,1)} %get-tuple-element.87) | copy-start | bytes 294916
  229.8 42.4 %copy-start.43 = (bf16[2,384,768]{2,1,0:T(8,128)(2,1)S(1)}, bf16[2,384,768]{2,1,0:T(8,128)(2,1)}, u32[]{:S(2)}) copy-start(bf16[2,384,768]{2,1,0:T(8,128)(2,1)} %get-tuple-element.61) | copy-start | bytes 3538948
  315.0 2.6 copy-start.3
  315.0 2.6 copy-start.5
  315.0 2.6 copy-start.33
  317.6 3.8 %copy-start.51 = (f32[8,32]{1,0:T(8,128)S(1)}, f32[8,32]{1,0:T(8,128)}, u32[]{:S(2)}) copy-start(f32[8,32]{1,0:T(8,128)} %get-tuple-element.96) | copy-start | bytes 3076
  317.6 4.4 %copy-start.30 = (bf16[4,96,576]{2,1,0:T(8,128)(2,1)S(1)}, bf16[4,96,576]{2,1,0:T(8,128)(2,1)}, u32[]{:S(2)}) copy-start(bf16[4,96,576]{2,1,0:T(8,128)(2,1)} %get-tuple-element.99) | copy-start | bytes 1327108
  322.3 2.6 copy-start.37
  322.3 3.4 %copy-start.32 = (bf16[4,128,384]{2,1,0:T(8,128)(2,1)S(1)}, bf16[4,128,384]{2,1,0:T(8,128)(2,1)}, u32[]{:S(2)}) copy-start(bf16[4,128,384]{2,1,0:T(8,128)(2,1)} %get-tuple-element.103) | copy-start | bytes 1179652
  (21 other events, 36.1 us)
where the time goes:
time: 328 us; the launch traced here: 327 us
  Pallas kernels  249 us (76%)
  matrix products  30.4 us (9%)
  local copies, waits for them, and re-layouts  29.8 us (9%)
  other arithmetic  16.4 us (5%)
    pallas_call x8, Pallas kernels, call(): pl.pallas_call(body, out_shape=outs, in_specs=[vmem()] * len(inputs), out...  229 us
    pallas_call x4, Pallas kernels, local_call(): pl.pallas_call(kernel, out_shape=outs, in_specs=[vmem()] * len(inputs), o...  20 us
    dot_general x9, matrix products, mm(): return jnp.dot(left, right, preferred_element_type=F32)  13 us
    unnamed x118, local copies, waits for them, and re-layouts  12.5 us
    dot_general x9, matrix products, mm_nt(): lax.dot_general(left, right, (((1,), (1,)), ((), ())), preferred_element_...  10.5 us

commit v1 on v0

v1 whole, which is shorter than its diff:
```python
import functools
import itertools

import jax
import jax.numpy as jnp
from jax import lax
from jax.experimental import pallas as pl
from jax.experimental.pallas import tpu as pltpu
from jax.sharding import PartitionSpec as P

EPSILON = 1e-06
MASKED = -1e30
MESH = pl.DeviceIdType.MESH
BF16 = jnp.bfloat16
F32 = jnp.float32


def low(values):
    return values.astype(BF16)


def mm(left, right):
    return jnp.dot(left, right, preferred_element_type=F32)


def mm_tn(left, right):
    return lax.dot_general(
        left, right, (((0,), (0,)), ((), ())), preferred_element_type=F32
    )


def mm_nt(left, right):
    return lax.dot_general(
        left, right, (((1,), (1,)), ((), ())), preferred_element_type=F32
    )


def vmem():
    return pl.BlockSpec(memory_space=pltpu.VMEM)


def inv_rms(rows):
    return lax.rsqrt(jnp.mean(rows * rows, axis=-1, keepdims=True) + EPSILON)


def norm_back(rows, gain, grad):
    r = inv_rms(rows)
    weighted = gain * grad
    d_gain = jnp.sum(grad * rows * r, axis=0, keepdims=True)
    d_rows = r * weighted - rows * (r * r * r) * jnp.mean(weighted * rows, axis=-1, keepdims=True)
    return d_rows, d_gain


class Wire:
    def __init__(self, sizes, send_sem, recv_sem):
        self.sizes = sizes
        self.send_sem, self.recv_sem = send_sem, recv_sem
        self.used = 0

    def peers(self, kind):
        ns, nc = self.sizes["shard"], self.sizes["context"]
        if isinstance(kind, tuple):
            a, n = kind[1], self.sizes[kind[1]]
            me = lax.axis_index(a)
            return [{a: lax.rem(me + o, n)} for o in range(1, n)]
        ms, mc = lax.axis_index("shard"), lax.axis_index("context")
        hi, lo = mc // 2, lax.rem(mc, 2)
        if kind == "sibling":
            return [{"context": 2 * hi + 1 - lo}]
        if kind == "hi":
            return [{"context": 2 * lax.rem(hi + o, nc // 2) + lo} for o in range(1, nc // 2)]
        if kind == "apart":
            offs = [o for o in itertools.product(range(ns), range(nc // 2)) if any(o)]
            return [
                {"shard": lax.rem(ms + o, ns), "context": 2 * lax.rem(hi + p, nc // 2) + lo}
                for o, p in offs
            ]
        offs = [o for o in itertools.product(range(ns), range(nc)) if any(o)]
        return [{"shard": lax.rem(ms + o, ns), "context": lax.rem(mc + p, nc)} for o, p in offs]

    def barrier(self, kinds):
        sem = pltpu.get_barrier_semaphore()
        count = 0
        for kind in dict.fromkeys(kinds):
            for peer in self.peers(kind):
                pl.semaphore_signal(sem, inc=1, device_id=peer, device_id_type=MESH)
                count += 1
        pl.semaphore_wait(sem, count)

    def send(self, kind, source, target):
        copies = []
        for k, peer in enumerate(self.peers(kind)):
            copies.append(self.one(peer, source(peer), target(k)))
        return copies

    def one(self, peer, source, target):
        copy = pltpu.make_async_remote_copy(
            src_ref=source,
            dst_ref=target,
            send_sem=self.send_sem.at[self.used],
            recv_sem=self.recv_sem.at[self.used],
            device_id=peer,
            device_id_type=MESH,
        )
        copy.start()
        self.used += 1
        return copy


def wait_recv(copies):
    for copy in copies:
        copy.wait_recv()


def wait_send(copies):
    for copy in copies:
        copy.wait_send()


def n_peers(sizes, kind):
    if isinstance(kind, tuple):
        return sizes[kind[1]] - 1
    ns, nc = sizes["shard"], sizes["context"]
    return {"sibling": 1, "hi": nc // 2 - 1, "apart": ns * nc // 2 - 1, "group": ns * nc - 1}[kind]


def call(cid, sizes, body, inputs, outs, scratch, copies):
    return pl.pallas_call(
        body,
        out_shape=outs,
        in_specs=[vmem()] * len(inputs),
        out_specs=tuple(vmem() for _ in outs),
        scratch_shapes=list(scratch)
        + [pltpu.SemaphoreType.DMA((copies,)), pltpu.SemaphoreType.DMA((copies,))],
        compiler_params=pltpu.CompilerParams(collective_id=cid, has_side_effects=True),
    )(*inputs)


def comm(cid, sizes, gathers, sums, reduces, epilogue, extra_in, extra_out, smalls=()):
    ns, nc = sizes["shard"], sizes["context"]
    nh = nc // 2
    ng, nsum, nr, nx, nsm = len(gathers), len(sums), len(reduces), len(extra_in), len(smalls)
    inputs = [g for g, _ in gathers] + list(sums) + [r for r, _ in reduces] + list(extra_in)
    inputs += [s for s, _ in smalls]
    outs, copies, kinds = [], 0, []
    for g, how in gathers:
        if how == "shard":
            outs.append(jax.ShapeDtypeStruct((ns,) + g.shape, g.dtype))
            copies += 2 * (ns - 1)
            kinds += [("axis", "shard"), "sibling"]
        elif how == "context":
            outs.append(jax.ShapeDtypeStruct((nh, 2) + g.shape, g.dtype))
            copies += 1 + 2 * (nh - 1)
            kinds += ["hi", "sibling"]
        else:
            axis = how.split(":")[1]
            outs.append(jax.ShapeDtypeStruct((sizes[axis],) + g.shape, g.dtype))
            copies += sizes[axis] - 1
            kinds.append(("axis", axis))
    outs += [jax.ShapeDtypeStruct(s.shape[1:], BF16) for s in sums]
    apart = n_peers(sizes, "apart")
    copies += nsum * (1 + apart + 1 + 2 * (nh - 1))
    kinds += ["sibling", "apart", "hi"] if nsum else []
    second = epilogue.second if epilogue else []
    outs += [jax.ShapeDtypeStruct((sizes[ax],) + shape, dt) for ax, shape, dt in second]
    axes = [a for _, a in reduces] + [ax for ax, _, _ in second]
    copies += sum(sizes[a] - 1 for a in axes)
    kinds += [("axis", a) for a in axes]
    outs += list(extra_out)
    outs += [jax.ShapeDtypeStruct(s.shape, F32) for s, _ in smalls]
    copies += sum(n_peers(sizes, kind) for _, kind in smalls)
    kinds += [kind for _, kind in smalls]
    scratch = []
    for s in sums:
        scratch += [
            pltpu.VMEM((ns,) + s.shape[2:], BF16),
            pltpu.VMEM((ns,) + s.shape[2:], BF16),
            pltpu.VMEM((apart,) + s.shape[3:], BF16),
        ]
    scratch += [pltpu.VMEM((sizes[a] - 1,) + r.shape[1:], r.dtype) for r, a in reduces]
    scratch += [pltpu.VMEM((n_peers(sizes, kind),) + s.shape, F32) for s, kind in smalls]
    n_in, n_out = len(inputs), len(outs)

    def body(*refs):
        ins, os_ = refs[:n_in], refs[n_in : n_in + n_out]
        scr, (send_sem, recv_sem) = refs[n_in + n_out : -2], refs[-2:]
        g_in, s_in = ins[:ng], ins[ng : ng + nsum]
        r_in = ins[ng + nsum : ng + nsum + nr]
        x_in = ins[ng + nsum + nr : ng + nsum + nr + nx]
        sm_in = ins[ng + nsum + nr + nx :]
        g_out, s_out = os_[:ng], os_[ng : ng + nsum]
        e_out = os_[ng + nsum : ng + nsum + len(second)]
        x_out = os_[ng + nsum + len(second) : n_out - nsm]
        sm_out = os_[n_out - nsm :]
        s_scr = [scr[3 * i : 3 * i + 3] for i in range(nsum)]
        r_land, sm_land = scr[3 * nsum : 3 * nsum + nr], scr[3 * nsum + nr :]
        ms, mc = lax.axis_index("shard"), lax.axis_index("context")
        hi, lo = mc // 2, lax.rem(mc, 2)
        sibling = {"context": 2 * hi + 1 - lo}
        wire = Wire(sizes, send_sem, recv_sem)
        wire.barrier(kinds)
        pending, recvs, forwards = [], [], []

        r_copies = [
            wire.send(
                ("axis", a), lambda p, ref=ref, a=a: ref.at[p[a]], lambda k, land=land: land.at[k]
            )
            for ref, land, (_, a) in zip(r_in, r_land, reduces)
        ]
        s_first = [wire.one(sibling, ref.at[:, 1 - lo], l[0]) for ref, l in zip(s_in, s_scr)]
        for ref, out, (_, how) in zip(g_in, g_out, gathers):
            if how == "shard":
                c = wire.send(
                    ("axis", "shard"),
                    lambda p, ref=ref: ref.at[lo],
                    lambda k, out=out: out.at[ms, lo],
                )
                slots = [out.at[lax.rem(ms + ns - o, ns), lo] for o in range(1, ns)]
                forwards += list(zip(c, slots))
            elif how == "context":
                c = wire.send(
                    "hi", lambda p, ref=ref: ref, lambda k, out=out: out.at[hi, lo]
                )
                slots = [out.at[lax.rem(hi + nh - o, nh), lo] for o in range(1, nh)]
                forwards += list(zip(c, slots))
                own = wire.one(sibling, ref, out.at[hi, lo])
                recvs.append(own)
                pending.append(own)
            else:
                axis = how.split(":")[1]
                me = lax.axis_index(axis)
                c = wire.send(
                    ("axis", axis),
                    lambda p, ref=ref: ref,
                    lambda k, out=out, me=me: out.at[me],
                )
                recvs += c
            pending += c
        for ref, out, (_, how) in zip(g_in, g_out, gathers):
            if how == "shard":
                out[ms] = ref[...]
            elif how == "context":
                out[hi, lo] = ref[...]
            else:
                out[lax.axis_index(how.split(":")[1])] = ref[...]

        s_second = []
        for ref, c, (land, pair, others) in zip(s_in, s_first, s_scr):
            c.wait_recv()
            for i in range(ns):
                pair[i] = low(ref[i, lo].astype(F32) + land[i].astype(F32))
            s_second.append(
                wire.send(
                    "apart",
                    lambda p, pair=pair: pair.at[p["shard"], p["context"] // 2],
                    lambda k, others=others: others.at[k],
                )
            )
            pending.append(c)

        totals = []
        for ref, land, c, (_, a) in zip(r_in, r_land, r_copies, reduces):
            wait_recv(c)
            total = ref[lax.axis_index(a)].astype(F32)
            for k in range(sizes[a] - 1):
                total = total + land[k].astype(F32)
            totals.append(total)
            pending += c
        if epilogue is not None:
            blocks = epilogue.run(totals, x_in, x_out)
            for block, out, (ax, _, _) in zip(blocks, e_out, second):
                mine = lax.axis_index(ax)
                out[mine] = block
                c = wire.send(
                    ("axis", ax),
                    lambda p, out=out, mine=mine: out.at[mine],
                    lambda k, out=out, mine=mine: out.at[mine],
                )
                pending += c
                recvs += c

        for c, slot in forwards:
            c.wait_recv()
            f = wire.one(sibling, slot, slot)
            pending.append(f)
            recvs.append(f)
        forwards = []
        for c, (land, pair, others), out in zip(s_second, s_scr, s_out):
            wait_recv(c)
            pending += c
            total = pair[ms, hi].astype(F32)
            for k in range(apart):
                total = total + others[k].astype(F32)
            out[lo, hi] = low(total)
            c2 = wire.send(
                "hi", lambda p, out=out: out.at[lo, hi], lambda k, out=out: out.at[lo, hi]
            )
            pending += c2
            forwards += [
                (c3, out.at[lo, lax.rem(hi + nh - o, nh)]) for c3, o in zip(c2, range(1, nh))
            ]
            own = wire.one(sibling, out.at[lo, hi], out.at[lo, hi])
            pending.append(own)
            recvs.append(own)
        for i, (_, kind) in enumerate(smalls):
            source = epilogue.small_fill(i, sm_in, x_out, sm_out)
            land = sm_land[i]
            c = wire.send(kind, lambda p, src=source: src, lambda k, l=land: l.at[k])
            wait_recv(c)
            wait_send(c)
            total = source[...]
            for k in range(len(c)):
                total = total + land[k]
            sm_out[i][...] = total
        for c, slot in forwards:
            c.wait_recv()
            f = wire.one(sibling, slot, slot)
            pending.append(f)
            recvs.append(f)
        wait_recv(recvs)
        wait_send(pending)

    return call(cid, sizes, body, inputs, outs, scratch, copies)


class Epilogue:
    def __init__(self, second, run, small_fill=None):
        self.second, self.run, self.small_fill = second, run, small_fill


def one_hot(ids, values):
    row = lax.broadcasted_iota(jnp.int32, (8, ids.shape[1]), 0)
    wanted = row
    if values is not None:
        wanted = jnp.full_like(row, -1)
        for r, value in enumerate(values):
            wanted = jnp.where(row == r, value, wanted)
    return jnp.where(wanted == ids, 1.0, 0.0).astype(F32)


def same_doc(left, right):
    return mm_tn(left, right) > 0.5


def self_fwd_kernel(heads, dh, q, kv, seg_q, seg_k, line, mixed, probs):
    rows, span = probs.shape[1:]
    width = heads * dh
    first = lax.axis_index("context") * rows
    t = first + lax.broadcasted_iota(jnp.int32, (rows, span), 0)
    u = lax.broadcasted_iota(jnp.int32, (rows, span), 1)
    allowed = (u <= t) & same_doc(one_hot(seg_q[...], None), one_hot(seg_k[...], None))
    for h in range(heads):
        cols = slice(h * dh, (h + 1) * dh)
        bias = pltpu.roll(
            jnp.broadcast_to(line[h : h + 1, :], (rows, span)), 0, 1, stride=1, stride_axis=0
        )
        s = mm_nt(q[:, cols], kv[:, cols]) + bias
        s = jnp.where(allowed, s, MASKED)
        e = jnp.exp(s - jnp.max(s, axis=1, keepdims=True))
        p = e / jnp.sum(e, axis=1, keepdims=True)
        probs[h] = p
        mixed[:, cols] = low(mm(low(p), kv[:, width + h * dh : width + (h + 1) * dh]))


def cross_fwd_kernel(heads, dh, q, kv, seg_q, seg_k, source, mixed, probs):
    width = heads * dh
    docs = [source[0, d] for d in range(source.shape[1])]
    allowed = same_doc(one_hot(seg_q[...], None), one_hot(seg_k[...], docs))
    for h in range(heads):
        cols = slice(h * dh, (h + 1) * dh)
        s = jnp.where(allowed, mm_nt(q[:, cols], kv[:, cols]), MASKED)
        e = jnp.exp(s - jnp.max(s, axis=1, keepdims=True))
        p = e / jnp.sum(e, axis=1, keepdims=True)
        probs[h] = p
        mixed[:, cols] = low(mm(low(p), kv[:, width + h * dh : width + (h + 1) * dh]))


def back_kernel(heads, dh, with_bias, q, kv, probs, g, dq, dkv, *diag):
    rows, span = probs.shape[1:]
    width = heads * dh
    if with_bias:
        a = lax.broadcasted_iota(jnp.int32, (rows, rows), 0)
        b = lax.broadcasted_iota(jnp.int32, (rows, rows), 1)
        flip = jnp.where(a + b == rows - 1, 1.0, 0.0).astype(BF16)
        diag[0][...] = jnp.zeros_like(diag[0])
    for h in range(heads):
        cols = slice(h * dh, (h + 1) * dh)
        vcols = slice(width + h * dh, width + (h + 1) * dh)
        p = probs[h]
        dp = mm_nt(g[:, cols], kv[:, vcols])
        ds = low(p * (dp - jnp.sum(dp * p, axis=1, keepdims=True)))
        dq[:, cols] = low(mm(ds, kv[:, cols]))
        dkv[:, cols] = low(mm_tn(ds, q[:, cols]))
        dkv[:, vcols] = low(mm_tn(low(p), g[:, cols]))
        if with_bias:
            skew = pltpu.roll(mm(flip, ds), 0, 1, stride=1, stride_axis=0)
            diag[0][h : h + 1, :] = jnp.sum(skew, axis=0, keepdims=True)


def local_call(kernel, inputs, outs, scalars=0):
    return pl.pallas_call(
        kernel,
        out_shape=outs,
        in_specs=[vmem()] * (len(inputs) - scalars)
        + [pl.BlockSpec(memory_space=pltpu.SMEM)] * scalars,
        out_specs=tuple(vmem() for _ in outs),
    )(*inputs)


def sds(shape, dtype):
    return jax.ShapeDtypeStruct(shape, dtype)


def body(
    sizes,
    hidden,
    enc_states,
    cotangent,
    segments,
    positions,
    enc_segments,
    doc_source,
    bucket_of,
    norm_self,
    norm_cross,
    norm_ffn,
    bias_table,
    w_q,
    w_k,
    w_v,
    w_o,
    c_q,
    c_k,
    c_v,
    c_o,
    w_gate,
    w_up,
    w_down,
):
    ns, nc, nt = sizes["shard"], sizes["context"], sizes["tensor"]
    seq_count, rows, width = hidden.shape
    assert seq_count == 1
    enc_len = enc_states.shape[1]
    heads = bias_table.shape[1]
    unit = w_q.shape[1]
    dh = unit // heads
    ffn = w_gate.shape[1]
    span = nc * rows
    enc_span = nc * enc_len
    ctx = lax.axis_index("context")
    part = rows // nt
    comm_ = functools.partial(comm, sizes=sizes)

    x = hidden[0]
    cot = cotangent[0]
    enc = enc_states[0]
    gain_s, gain_c, gain_f = norm_self[None, :], norm_cross[None, :], norm_ffn[None, :]

    def halves(array):
        return array.reshape(2, array.shape[0] // 2, array.shape[1])

    def columns(gathered):
        n, _, r, c = gathered.shape
        return jnp.moveaxis(gathered.reshape(n, 2 * r, c), 0, 1).reshape(2 * r, n * c)

    segs = jnp.concatenate([segments, enc_segments], axis=1)
    pack = jnp.concatenate([w_q.T, w_k.T, w_v.T], axis=0)
    qkv_all, seg_all = comm_(
        0,
        gathers=[(halves(pack), "shard"), (segs, "axis:context")],
        sums=[], reduces=[], epilogue=None, extra_in=[], extra_out=[],
    )
    w_qkv = columns(qkv_all)
    seg_k = seg_all[:, 0, :rows].reshape(1, span)
    enc_seg_k = seg_all[:, 0, rows:].reshape(1, enc_span)

    normed_self = low(x * inv_rms(x) * gain_s)
    qkv = low(mm_nt(normed_self, w_qkv))
    q = qkv[:, :unit]
    pack = jnp.concatenate([c_k.T, c_v.T, w_o], axis=0)
    kv_all, mid_all = comm_(
        1,
        gathers=[(qkv[:, unit:], "context"), (halves(pack), "shard")],
        sums=[], reduces=[], epilogue=None, extra_in=[], extra_out=[],
    )
    kv = kv_all.reshape(span, 2 * unit)
    mid_w = columns(mid_all)
    ckv, wo = mid_w[: 2 * unit], mid_w[2 * unit :]
    ekv_own = low(mm_nt(enc, ckv))

    flipped = bucket_of[::-1]
    twice = jnp.concatenate([flipped, flipped])
    bucket = lax.dynamic_slice(twice, (span - ctx * rows - 1,), (span,))
    onehot = (bucket[None, :] == jnp.arange(bias_table.shape[0], dtype=jnp.int32)[:, None]).astype(F32)
    line = lax.dot_general(
        bias_table, onehot, (((0,), (0,)), ((), ())), precision=lax.Precision.HIGHEST
    )
    mixed, probs = local_call(
        functools.partial(self_fwd_kernel, heads, dh),
        [q, kv, segments, seg_k, line],
        [sds((rows, unit), BF16), sds((heads, rows, span), F32)],
    )

    def fwd_step(totals, x_in, x_out):
        rows_in, gain = x_in
        base = rows_in[lax.axis_index("tensor")] if len(rows_in.shape) == 3 else rows_in[...]
        after = base + totals[0]
        x_out[0][...] = after
        return [low(after * inv_rms(after) * gain[...])]

    shape3 = (part, width)
    ep_fwd = Epilogue([("tensor", shape3, BF16)], fwd_step)
    part_self = low(mm(mixed, wo)).reshape(nt, part, width)
    pack = jnp.concatenate([c_q.T, c_o], axis=0)
    ekv_all, cqo_all, gate_all, up_all, normed_cross, after_self = comm_(
        2,
        gathers=[
            (ekv_own, "context"),
            (halves(pack), "shard"),
            (halves(w_gate), "shard"),
            (halves(w_up), "shard"),
        ],
        sums=[], reduces=[(part_self, "tensor")], epilogue=ep_fwd,
        extra_in=[x.reshape(nt, part, width), gain_c], extra_out=[sds(shape3, F32)],
    )
    ekv = ekv_all.reshape(enc_span, 2 * unit)
    cqo = columns(cqo_all)
    cq, co = cqo[:unit], cqo[unit:]
    wg, wu = gate_all.reshape(width, ffn), up_all.reshape(width, ffn)
    normed_cross = normed_cross.reshape(rows, width)

    cqs = low(mm_nt(normed_cross, cq))
    cmixed, cprobs = local_call(
        functools.partial(cross_fwd_kernel, heads, dh),
        [cqs, ekv, segments, enc_seg_k, doc_source],
        [sds((rows, unit), BF16), sds((heads, rows, enc_span), F32)],
        scalars=1,
    )
    part_cross = low(mm(cmixed, co)).reshape(nt, part, width)
    down_all, normed_ffn, after_cross = comm_(
        3,
        gathers=[(halves(w_down), "shard")],
        sums=[], reduces=[(part_cross, "tensor")], epilogue=ep_fwd,
        extra_in=[after_self, gain_f], extra_out=[sds(shape3, F32)],
    )
    wd = columns(down_all)
    normed_ffn = normed_ffn.reshape(rows, width)

    gate_pre, up_pre = mm(normed_ffn, wg), mm(normed_ffn, wu)
    top_low = low(cot)
    d_units = mm_nt(top_low, wd)
    k0, k1 = 0.7978845608028654, 0.044715
    sq = gate_pre * gate_pre
    th = jnp.tanh(k0 * (gate_pre + k1 * gate_pre * sq))
    gelu = 0.5 * gate_pre * (1.0 + th)
    d_gelu = 0.5 * (1.0 + th) + 0.5 * gate_pre * (1.0 - th * th) * k0 * (1.0 + 3.0 * k1 * sq)
    units = low(gelu * up_pre)
    d_gate = low(d_units * up_pre * d_gelu)
    d_up = low(d_units * gelu)
    part_out = low(mm(units, wd)).reshape(nt, part, width)
    part_ffn = low(mm_nt(d_gate, wg) + mm_nt(d_up, wu)).reshape(nt, part, width)

    def wide(grad):
        return low(grad).reshape(ns, 2, nc // 2, width // (ns * nc), grad.shape[1])

    def tall(grad):
        r, c = grad.shape
        return jnp.moveaxis(low(grad).reshape(2, nc // 2, r // nc, ns, c // ns), 3, 0)

    g_down = tall(mm_tn(units, top_low))
    g_gate = wide(mm_tn(normed_ffn, d_gate))
    g_up = wide(mm_tn(normed_ffn, d_up))

    def back_step(totals, x_in, x_out):
        rows_in, gain, above = x_in
        over = above[lax.axis_index("tensor")] if len(above.shape) == 3 else above[...]
        d_rows, d_gain = norm_back(rows_in[...], gain[...], totals[0])
        grad = over + d_rows
        x_out[0][...] = grad
        x_out[1][...] = d_gain
        return [low(grad)]

    ep_back = Epilogue([("tensor", shape3, BF16)], back_step)
    back_out = [sds(shape3, F32), sds((1, width), F32)]
    down_sum, cross_low_grad, cross_grad, dg_ffn = comm_(
        4,
        gathers=[], sums=[g_down], reduces=[(part_ffn, "tensor")], epilogue=ep_back,
        extra_in=[after_cross, gain_f, cot.reshape(nt, part, width)], extra_out=back_out,
    )
    cross_low_grad = cross_low_grad.reshape(rows, width)
    d_cmixed = low(mm_nt(cross_low_grad, co))
    d_cq, d_ekv = local_call(
        functools.partial(back_kernel, heads, dh, False),
        [cqs, ekv, cprobs, d_cmixed],
        [sds((rows, unit), BF16), sds((enc_span, 2 * unit), BF16)],
    )
    g_co = tall(mm_tn(cmixed, cross_low_grad))
    part_ncross = low(mm(d_cq, cq)).reshape(nt, part, width)

    def cross_back_step(totals, x_in, x_out):
        x_out[2][...] = low(totals[1])
        return back_step(totals, x_in, x_out)

    gate_sum, up_sum, co_sum, self_low_grad, self_grad, dg_cross, d_ekv_own = comm_(
        5,
        gathers=[], sums=[g_gate, g_up, g_co],
        reduces=[
            (part_ncross, "tensor"),
            (d_ekv.reshape(nc, enc_len, 2 * unit), "context"),
        ],
        epilogue=Epilogue([("tensor", shape3, BF16)], cross_back_step),
        extra_in=[after_self, gain_c, cross_grad],
        extra_out=back_out + [sds((enc_len, 2 * unit), BF16)],
    )
    self_low_grad = self_low_grad.reshape(rows, width)
    d_mixed = low(mm_nt(self_low_grad, wo))
    d_q, d_kv, diag = local_call(
        functools.partial(back_kernel, heads, dh, True),
        [q, kv, probs, d_mixed],
        [sds((rows, unit), BF16), sds((span, 2 * unit), BF16), sds((8, span), F32)],
    )

    g_wo = tall(mm_tn(mixed, self_low_grad))
    g_cq = tall(mm_tn(d_cq, normed_cross))
    g_ckv = tall(mm_tn(d_ekv_own, enc))
    part_enc = low(mm(d_ekv_own, ckv)).reshape(nt, enc_len // nt, width)

    def mid_step(totals, x_in, x_out):
        base = x_in[0][...] - x_in[1][lax.axis_index("tensor")]
        x_out[0][...] = low(totals[0])
        return [low(totals[1] + base), low(totals[2])]

    wo_sum, cq_sum, ckv_sum, out_delta, d_enc, d_kv_own = comm_(
        6,
        gathers=[], sums=[g_wo, g_cq, g_ckv],
        reduces=[
            (d_kv.reshape(nc, rows, 2 * unit), "context"),
            (part_out, "tensor"),
            (part_enc, "tensor"),
        ],
        epilogue=Epilogue(
            [("tensor", shape3, BF16), ("tensor", (enc_len // nt, width), BF16)], mid_step
        ),
        extra_in=[after_cross, x.reshape(nt, part, width)],
        extra_out=[sds((rows, 2 * unit), BF16)],
    )
    d_qkv = jnp.concatenate([d_q, d_kv_own], axis=1)
    part_nself = low(mm(d_qkv, w_qkv)).reshape(nt, part, width)
    g_self = tall(mm_tn(d_qkv, normed_self))

    bucket_d = lax.dynamic_slice(twice, (lax.rem(2 * span - ctx * rows - rows, span),), (span,))
    onehot_d = (bucket_d[None, :] == jnp.arange(bias_table.shape[0], dtype=jnp.int32)[:, None]).astype(F32)
    g_bias = lax.dot_general(
        diag, onehot_d, (((1,), (1,)), ((), ())), precision=lax.Precision.HIGHEST
    )

    def last_step(totals, x_in, x_out):
        rows_in, gain, above, cot_in, dgf, dgc = x_in
        d_rows, d_gain = norm_back(rows_in[lax.axis_index("tensor")], gain[...], totals[0])
        x_out[0][0:1, :] = dgf[...]
        x_out[0][1:2, :] = dgc[...]
        x_out[0][2:3, :] = d_gain
        x_out[0][3:8, :] = jnp.zeros_like(x_out[0][3:8, :])
        return [low(above[...] - cot_in[lax.axis_index("tensor")] + d_rows)]

    def small_fill(i, sm_in, x_out, sm_out):
        return [sm_in[0], x_out[0], sm_out[1]][i]

    gains0 = jnp.zeros((8, width), F32)
    self_sum, hid_delta, _, bias_sum, _, gain_sum = comm_(
        7,
        gathers=[], sums=[g_self], reduces=[(part_nself, "tensor")],
        epilogue=Epilogue([("tensor", shape3, BF16)], last_step, small_fill),
        extra_in=[
            x.reshape(nt, part, width), gain_s, self_grad, cot.reshape(nt, part, width),
            dg_ffn, dg_cross,
        ],
        extra_out=[sds((8, width), F32)],
        smalls=[(g_bias, "group"), (gains0, ("axis", "tensor")), (gains0, "group")],
    )

    def wide_out(total):
        return total.reshape(width // ns, total.shape[-1]).astype(F32)

    def tall_out(total):
        return total.reshape(-1, total.shape[-1]).astype(F32)

    self_w, ckv_w = tall_out(self_sum), tall_out(ckv_sum)
    return (
        (x + out_delta.reshape(rows, width).astype(F32))[None],
        (cot + hid_delta.reshape(rows, width).astype(F32))[None],
        d_enc.reshape(1, enc_len, width).astype(F32),
        gain_sum[2],
        gain_sum[1],
        gain_sum[0],
        bias_sum[:heads].T,
        self_w[:unit].T,
        self_w[unit : 2 * unit].T,
        self_w[2 * unit :].T,
        tall_out(wo_sum),
        tall_out(cq_sum).T,
        ckv_w[:unit].T,
        ckv_w[unit:].T,
        tall_out(co_sum),
        wide_out(gate_sum),
        wide_out(up_sum),
        tall_out(down_sum),
    )


def solution(mesh):
    tok = P("shard", "context", None)
    ids = P("shard", "context")
    wide, tall = P("shard", "tensor"), P("tensor", "shard")
    in_specs = (tok, tok, tok, ids, ids, ids, P("shard", None), P(), P(), P(), P(), P(None, "tensor"))
    in_specs += (wide, wide, wide, tall) * 2 + (wide, wide, tall)
    out_specs = (tok, tok, tok, P(), P(), P(), P(None, "tensor"))
    out_specs += (wide, wide, wide, tall) * 2 + (wide, wide, tall)
    sizes = {a: mesh.shape[a] for a in ("shard", "context", "tensor")}
    return jax.shard_map(
        functools.partial(body, sizes),
        mesh=mesh,
        in_specs=in_specs,
        out_specs=out_specs,
        check_vma=False,
    )
```

time: 328 us -> 280 us (0.85)
  Pallas kernels: 249 us -> 211 us
  matrix products: 30.4 us -> 25.2 us
    pallas_call x8, Pallas kernels: 229 us -> 191 us  [call(): pl.pallas_call(body, out_shape=outs, in_specs=[vmem()] * len(inputs), out...]
    unnamed x118 -> x97, local copies, waits for them, and re-layouts: 12.5 us -> 1.46 us
    reshape x10 -> x16, local copies, waits for them, and re-layouts: 4.47 us -> 14.2 us  [the longest x12 8.02 us: tall(): low(grad).reshape(2, nc // 2, r // nc, ns, c // ns)]
    dot_general x9 -> x8, matrix products: 10.5 us -> 5.98 us  [mm_nt(): lax.dot_general(left, right, (((1,), (1,)), ((), ())), preferred_element_...]
    dot_general x9 -> x8, matrix products: 13 us -> 10.5 us  [mm(): return jnp.dot(left, right, preferred_element_type=F32)]
where the time goes in v1:
time: 280 us; the launch traced here: 279 us
  Pallas kernels  211 us (75%)
  local copies, waits for them, and re-layouts  27.3 us (10%)
  matrix products  25.2 us (9%)
  other arithmetic  14.3 us (5%)
    pallas_call x8, Pallas kernels, call(): pl.pallas_call(body, out_shape=outs, in_specs=[vmem()] * len(inputs), out...  191 us
    pallas_call x4, Pallas kernels, local_call(): pl.pallas_call(kernel, out_shape=outs, in_specs=[vmem()] * (len(inputs) -...  19.5 us
    dot_general x8, matrix products, mm(): return jnp.dot(left, right, preferred_element_type=F32)  10.5 us
    reshape x12, local copies, waits for them, and re-layouts, tall(): low(grad).reshape(2, nc // 2, r // nc, ns, c // ns)  8.02 us
    dot_general x8, matrix products, mm_tn(): lax.dot_general(left, right, (((0,), (0,)), ((), ())), preferred_element_...  6.5 us
    reshape x4, local copies, waits for them, and re-layouts, columns(): gathered.reshape(n, 2 * r, c)  6.14 us
    dot_general x8, matrix products, mm_nt(): lax.dot_general(left, right, (((1,), (1,)), ((), ())), preferred_element_...  5.98 us

profile of v1, /device:TPU:0, one launch (start us, length us, event | category | flops | bytes accessed | tf_op | source)
XLA Modules:
  0.0 278.8 jit_solution(17551813171876480995)
XLA Ops:
  1.6 1.5 convolution_bitcast_fusion.1.line
  3.0 1.9 pad_maximum_fusion
  4.9 1.3 pad_add_fusion.refs_1_
  6.1 13.4 %shard_map.349 = (bf16[2,2,288,384]{3,2,1,0:T(8,128)(2,1)}, s32[4,1,384]{2,1,0:T(1,128)}) custom-call(bf16[2,288,384]{2,1,0:T(8,128)(2,1)} %bitcast.228, s32[1,384]{1,0:T(1,128)} %pad_add_fusion.refs_1_), custom_call_target="tpu_custom_call" | custom-call | tf_op jit(solution)/shard_map/pallas_call | solution.py:128
  19.5 2.2 copy.75
  24.5 11.2 %shard_map.350 = (bf16[2,2,256,384]{3,2,1,0:T(8,128)(2,1)}, bf16[2,2,288,384]{3,2,1,0:T(8,128)(2,1)}) custom-call(bf16[256,384]{1,0:T(8,128)(2,1)} %slice.93.refs_0_, bf16[2,288,384]{2,1,0:T(8,128)(2,1)} %bitcast.227), custom_call_target="tpu_custom_call" | custom-call | tf_op jit(solution)/shard_map/pallas_call | solution.py:128
  37.0 5.3 %shard_map.351 = (bf16[256,192]{1,0:T(8,128)(2,1)}, f32[3,256,1024]{2,1,0:T(8,128)}) custom-call(bf16[256,192]{1,0:T(8,128)(2,1)} %slice.92.q, bf16[1024,384]{1,0:T(8,128)(2,1)} %bitcast.214, s32[1,256]{1,0:T(1,128)} %seg_q.3, s32[1,1024]{1,0:T(1,128)} %bitcast.272, f32[3,1024]{1,0:T(4,128)} %convolution_bitcast_fusion.1.line), custom_call_target="tpu_custom_call" | custom-call | tf_op jit(solution)/shard_map/pallas_call | solution.py:401
  46.6 23.5 %shard_map.352 = (bf16[2,2,128,384]{3,2,1,0:T(8,128)(2,1)}, bf16[2,2,192,384]{3,2,1,0:T(8,128)(2,1)}, bf16[2,2,192,512]{3,2,1,0:T(8,128)(2,1)}, bf16[2,2,192,512...) custom-call(bf16[128,384]{1,0:T(8,128)(2,1)} %fusion.1.refs_0_, bf16[2,192,384]{2,1,0:T(8,128)(2,1)} %bitcast.245, ...), custom_call_target="tpu_custom_call" | custom-call | tf_op jit(solution)/shard_map/pallas_call | solution.py:128
  70.1 1.7 copy.117
  73.8 3.7 %shard_map.353 = (bf16[256,192]{1,0:T(8,128)(2,1)}, f32[3,256,512]{2,1,0:T(8,128)}) custom-call(bf16[256,192]{1,0:T(8,128)(2,1)} %convolution_convert_fusion.15.q, bf16[512,384]{1,0:T(8,128)(2,1)} %bitcast.240, s32[1,256]{1,0:T(1,128)} %seg_q.3, s32[1,512]{1,0:T(1,128)} %slice_bitcast_fusion.4.seg_k, s32[1,3]{1,0:T(1,128)} %source.1), custom_call_target="tpu_custom_call" | custom-call | tf_op jit(solution)/shard_map/pallas_call | solution.py:401
  77.6 2.0 convolution_convert_fusion.8
  80.2 25.0 %shard_map.354 = (bf16[2,2,256,384]{3,2,1,0:T(8,128)(2,1)}, bf16[4,64,768]{2,1,0:T(8,128)(2,1)}, f32[64,768]{1,0:T(8,128)}) custom-call(bf16[2,256,384]{2,1,0:T(8,128)(2,1)} %bitcast.259, bf16[4,64,768]{2,1,0:T(8,128)(2,1)} %bitcast.238, f32[64,768]{1,0:T(8,128)} %get-tuple-element.70.refs_2_.refs_5_, f32[1,768]{1,0:T(1,128)} %broadcast_in_dim.9.refs_3_), custom_call_target="tpu_custom_call" | custom-call | tf_op jit(solution)/shard_map/pallas_call | solution.py:128
  105.2 1.5 copy.82
  110.6 1.3 convolution_convert_fusion.1
  111.8 2.3 reshape.268
  115.1 23.2 %shard_map.355 = (bf16[2,2,128,384]{3,2,1,0:T(8,128)(2,1)}, bf16[4,64,768]{2,1,0:T(8,128)(2,1)}, f32[64,768]{1,0:T(8,128)}, f32[1,768]{1,0:T(1,128)}) custom-call(bf16[2,2,2,128,384]{4,3,2,1,0:T(8,128)(2,1)} %bitcast.218, bf16[4,64,768]{2,1,0:T(8,128)(2,1)} %bitcast.239, f32[64,768]{1,0:T(8,128)} %get-tuple-element.75.refs_2_.refs_6_, ...), custom_call_target="tpu_custom_call" | custom-call | tf_op jit(solution)/shard_map/pallas_call | solution.py:128
  138.3 1.3 convolution_convert_fusion.18
  140.4 4.2 %shard_map.356 = (bf16[256,192]{1,0:T(8,128)(2,1)}, bf16[512,384]{1,0:T(8,128)(2,1)}) custom-call(bf16[256,192]{1,0:T(8,128)(2,1)} %convolution_convert_fusion.15.q, bf16[512,384]{1,0:T(8,128)(2,1)} %bitcast.241, f32[3,256,512]{2,1,0:T(8,128)} %get-tuple-element.77.probs, bf16[256,192]{1,0:T(8,128)(2,1)} %copy.92.g), custom_call_target="tpu_custom_call" | custom-call | tf_op jit(solution)/shard_map/pallas_call | solution.py:401
  144.6 1.9 convolution_convert_fusion.7
  147.6 2.2 convolution_convert_fusion.2
  149.9 1.3 convolution_convert_fusion.3
  151.2 29.3 %shard_map.357 = (bf16[2,2,96,512]{3,2,1,0:T(8,128)(2,1)}, bf16[2,2,96,512]{3,2,1,0:T(8,128)(2,1)}, bf16[2,2,48,384]{3,2,1,0:T(8,128)(2,1)}, bf16[4,64,768]{2,1,...) custom-call(bf16[2,2,2,96,512]{4,3,2,1,0:T(8,128)(2,1)} %bitcast.220, ...), custom_call_target="tpu_custom_call" | custom-call | tf_op jit(solution)/shard_map/pallas_call | solution.py:128
  180.5 2.5 bitcast_convert_fusion.2
  184.0 1.2 convolution_convert_fusion.6
  186.3 6.4 %shard_map.358 = (bf16[256,192]{1,0:T(8,128)(2,1)}, bf16[1024,384]{1,0:T(8,128)(2,1)}, f32[8,1024]{1,0:T(8,128)}) custom-call(bf16[256,192]{1,0:T(8,128)(2,1)} %slice.92.q, bf16[1024,384]{1,0:T(8,128)(2,1)} %bitcast.215, f32[3,256,1024]{2,1,0:T(8,128)} %get-tuple-element.83.probs, bf16[256,192]{1,0:T(8,128)(2,1)} %copy.96.g), custom_call_target="tpu_custom_call" | custom-call | tf_op jit(solution)/shard_map/pallas_call | solution.py:401
  196.3 34.5 %shard_map.359 = (bf16[2,2,48,384]{3,2,1,0:T(8,128)(2,1)}, bf16[2,2,48,384]{3,2,1,0:T(8,128)(2,1)}, bf16[2,2,96,384]{3,2,1,0:T(8,128)(2,1)}, bf16[4,64,768]{2,1,...) custom-call(bf16[2,2,2,48,384]{4,3,2,1,0:T(8,128)(2,1)} %bitcast.244, ...), custom_call_target="tpu_custom_call" | custom-call | tf_op jit(solution)/shard_map/pallas_call | solution.py:128
  230.8 1.9 convert_bitcast_fusion
  232.7 2.2 convolution_convert_fusion.5
  238.7 31.0 %shard_map.360 = (bf16[2,2,144,384]{3,2,1,0:T(8,128)(2,1)}, bf16[4,64,768]{2,1,0:T(8,128)(2,1)}, f32[8,768]{1,0:T(8,128)}, f32[8,32]{1,0:T(8,128)}, f32[8,768]{1,0:T(8,128)}, /*index=5*/f32[8,768]{1,0:T(8,128)}) custom-call(bf16[2,2,2,144,384]{4,3,2,1,0:T(8,128)(2,1)} %bitcast.208, bf16[4,64,768]{2,1,0:T(8,128)(2,1)} %bitcast.260, f32[4,64,768]{2,1,0:T(8,128)} %bitcast.195, ...), custom_call_target="tpu_custom_call" | custom-call | tf_op jit(solution)/shard_map/pallas_call | solution.py:128
  269.8 1.2 bitcast_convert_fusion
  272.1 1.3 convert_add_fusion
  273.3 1.5 slice_reduce_fusion
  (151 shorter events, 32.8 us)
Async XLA Ops:
  0.7 43.7 %copy-start = (bf16[1,128,768]{2,1,0:T(8,128)(2,1)S(1)}, bf16[1,128,768]{2,1,0:T(8,128)(2,1)}, u32[]{:S(2)}) copy-start(bf16[1,128,768]{2,1,0:T(8,128)(2,1)} %param.24) | copy-start | bytes 589828
  19.5 2.3 copy-start.1
  22.9 13.5 %copy-start.43 = (s32[4,1,384]{2,1,0:T(1,128)S(1)}, s32[4,1,384]{2,1,0:T(1,128)}, u32[]{:S(2)}) copy-start(s32[4,1,384]{2,1,0:T(1,128)} %get-tuple-element.63) | copy-start | bytes 18436
  35.8 6.5 %copy-start.22 = (bf16[2,2,288,384]{3,2,1,0:T(8,128)(2,1)S(1)}, bf16[2,2,288,384]{3,2,1,0:T(8,128)(2,1)}, u32[]{:S(2)}) copy-start(bf16[2,2,288,384]{3,2,1,0:T(8,128)(2,1)} %get-tuple-element.65) | copy-start | bytes 2654212
  43.2 2.1 copy-start.44
  43.2 2.7 copy-start.38
  43.2 2.7 copy-start.39
  70.1 2.2 copy-start.12
  72.2 7.4 %copy-start.45 = (f32[768]{0:T(1024)S(1)}, f32[768]{0:T(1024)}, u32[]{:S(2)}) copy-start(f32[768]{0:T(1024)} %param.32) | copy-start | bytes 9220
  77.6 27.6 %copy-start.10 = (bf16[24,8,2,384]{3,1,2,0:T(8,128)(2,1)}, bf16[24,8,2,384]{3,1,2,0:T(8,128)(2,1)S(1)}, u32[]{:S(2)}) copy-start(bf16[24,8,2,384]{3,1,2,0:T(8,128)(2,1)S(1)} %copy.106) | copy-start | bytes 884740
  77.6 29.1 %copy-start.4 = (f32[1,256,768]{2,1,0:T(8,128)S(1)}, f32[1,256,768]{2,1,0:T(8,128)}, u32[]{:S(2)}) copy-start(f32[1,256,768]{2,1,0:T(8,128)} %param.25) | copy-start | bytes 2359300
  115.1 23.2 %copy-start.11 = (bf16[24,8,2,384]{3,1,2,0:T(8,128)(2,1)S(1)}, bf16[24,8,2,384]{3,1,2,0:T(8,128)(2,1)}, u32[]{:S(2)}) copy-start(bf16[24,8,2,384]{3,1,2,0:T(8,128)(2,1)} %copy-done.10) | copy-start | bytes 884740
  140.4 6.1 %copy-start.15 = (bf16[4,64,768]{2,1,0:T(8,128)(2,1)S(1)}, bf16[4,64,768]{2,1,0:T(8,128)(2,1)}, u32[]{:S(2)}) copy-start(bf16[4,64,768]{2,1,0:T(8,128)(2,1)} %get-tuple-element.76) | copy-start | bytes 1179652
  140.4 6.1 %copy-start.27 = (bf16[256,192]{1,0:T(8,128)(2,1)S(1)}, bf16[256,192]{1,0:T(8,128)(2,1)}, u32[]{:S(2)}) copy-start(bf16[256,192]{1,0:T(8,128)(2,1)} %get-tuple-element.69) | copy-start | bytes 294916
  146.5 3.3 %copy-start.20 = (bf16[256,512]{0,1:T(8,128)(2,1)S(1)}, bf16[256,512]{0,1:T(8,128)(2,1)}, u32[]{:S(2)}) copy-start(bf16[256,512]{0,1:T(8,128)(2,1)} %copy-done.19) | copy-start | bytes 786436
  180.5 2.5 copy-start.28
  180.5 3.5 %copy-start.18 = (bf16[256,512]{0,1:T(8,128)(2,1)S(1)}, bf16[256,512]{0,1:T(8,128)(2,1)}, u32[]{:S(2)}) copy-start(bf16[256,512]{0,1:T(8,128)(2,1)} %copy-done.17) | copy-start | bytes 786436
  183.0 2.2 copy-start.14
  193.2 2.0 copy-start.25
  196.3 36.4 %copy-start.7 = (bf16[72,8,2,384]{3,1,2,0:T(8,128)(2,1)S(1)}, bf16[72,8,2,384]{3,1,2,0:T(8,128)(2,1)}, u32[]{:S(2)}) copy-start(bf16[72,8,2,384]{3,1,2,0:T(8,128)(2,1)} %copy-done.6) | copy-start | bytes 2654212
  196.3 36.4 %copy-start.40 = (bf16[256,192]{1,0:T(8,128)(2,1)S(1)}, bf16[256,192]{1,0:T(8,128)(2,1)}, u32[]{:S(2)}) copy-start(bf16[256,192]{1,0:T(8,128)(2,1)} %get-tuple-element.86) | copy-start | bytes 294916
  230.8 4.1 %copy-start.2 = (f32[1,256,768]{2,1,0:T(8,128)S(1)}, f32[1,256,768]{2,1,0:T(8,128)}, u32[]{:S(2)}) copy-start(f32[1,256,768]{2,1,0:T(8,128)} %param.23) | copy-start | bytes 2359300
  230.8 4.1 %copy-start.32 = (bf16[256,384]{1,0:T(8,128)(2,1)S(1)}, bf16[256,384]{1,0:T(8,128)(2,1)}, u32[]{:S(2)}) copy-start(bf16[256,384]{1,0:T(8,128)(2,1)} %get-tuple-element.87) | copy-start | bytes 589828
  269.8 2.2 copy-start.3
  269.8 2.2 copy-start.5
  269.8 2.2 copy-start.30
  269.8 2.2 copy-start.31
  272.0 2.8 %copy-start.46 = (f32[8,32]{1,0:T(8,128)S(1)}, f32[8,32]{1,0:T(8,128)}, u32[]{:S(2)}) copy-start(f32[8,32]{1,0:T(8,128)} %get-tuple-element.95) | copy-start | bytes 3076
  272.0 3.4 %copy-start.16 = (bf16[2,2,96,384]{3,2,1,0:T(8,128)(2,1)S(1)}, bf16[2,2,96,384]{3,2,1,0:T(8,128)(2,1)}, u32[]{:S(2)}) copy-start(bf16[2,2,96,384]{3,2,1,0:T(8,128)(2,1)} %get-tuple-element.99) | copy-start | bytes 884740
  272.0 4.2 %copy-start.33 = (bf16[4,32,768]{2,1,0:T(8,128)(2,1)S(1)}, bf16[4,32,768]{2,1,0:T(8,128)(2,1)}, u32[]{:S(2)}) copy-start(bf16[4,32,768]{2,1,0:T(8,128)(2,1)} %get-tuple-element.93) | copy-start | bytes 589828
  273.3 3.7 %copy-start.37 = (bf16[2,2,48,384]{3,2,1,0:T(8,128)(2,1)S(1)}, bf16[2,2,48,384]{3,2,1,0:T(8,128)(2,1)}, u32[]{:S(2)}) copy-start(bf16[2,2,48,384]{3,2,1,0:T(8,128)(2,1)} %get-tuple-element.100) | copy-start | bytes 442372
  273.3 4.5 %copy-start.29 = (bf16[2,2,128,384]{3,2,1,0:T(8,128)(2,1)S(1)}, bf16[2,2,128,384]{3,2,1,0:T(8,128)(2,1)}, u32[]{:S(2)}) copy-start(bf16[2,2,128,384]{3,2,1,0:T(8,128)(2,1)} %get-tuple-element.103) | copy-start | bytes 1179652
  (15 other events, 22.6 us)
